TPU v7x, 256 devices: a whole 4x4x8 slice. The times are simulated.
256 devices in a mesh: client: 32 (over x, z), feat: 8 (over y, core).
Axes of the slice: x: 4, y: 4, z: 8, core: 2. Of those that a mesh axis runs over, the one named last changes fastest.
Arguments:
- bin_codes: int32 [512, 49152], P('feat', 'client'), may hold values from 0 to 255
- node_ids: int32 [49152], P('client'), may hold values from 0 to 7
- margins: float32 [16, 49152], P(None, 'client'), may hold values from -1 to 3
- labels: float32 [16, 49152], P(None, 'client'), may hold values from 0 to 1
- split_feature: int32 [8], replicated, may hold values from 0 to 511
- split_bin: int32 [8], replicated, may hold values from 0 to 254
Outputs:
- split_gains: float32 [8, 512, 256], P(None, ('feat', 'client'))
- leaf_weights: float32 [16, 16], replicated
- new_margins: float32 [16, 49152], P(None, 'client')
All inputs are finite; a program needn't handle non-finite values.
Results may differ from a plain program's by a relative error of at most 0.0039.
Values may be sent and summed in bfloat16 or wider, within the bound.
A program may use at most 64 MiB of HBM per device.

v0:
```python
import math

import jax
import jax.numpy as jnp
from jax import lax
from jax.sharding import PartitionSpec as P

BINS = 256


reg_lambda = 1.0
step_eta = 0.5


def gain_table(prefix, targets):
    left_grad = prefix[..., :targets]
    left_hess = prefix[..., targets:]
    total_grad = prefix[:, -1:, :, :targets]
    total_hess = prefix[:, -1:, :, targets:]
    value = left_grad * left_grad / (left_hess + reg_lambda)
    value = value + (total_grad - left_grad) ** 2 / (total_hess - left_hess + reg_lambda)
    value = value - total_grad * total_grad / (total_hess + reg_lambda)
    return 0.5 * jnp.sum(value, axis=-1)


def leaf_table(left_sums, node_sums, targets):
    left_grad = left_sums[:, :targets]
    left_hess = left_sums[:, targets:]
    total_grad = node_sums[:, :targets]
    total_hess = node_sums[:, targets:]
    left_weight = -left_grad / (left_hess + reg_lambda)
    right_weight = -(total_grad - left_grad) / (total_hess - left_hess + reg_lambda)
    return jnp.stack([left_weight, right_weight], axis=1).reshape(2 * left_sums.shape[0], targets)


def expand(row_stats, node_list, node_total):
    node_mask = (node_list[:, None] == jnp.arange(node_total, dtype=jnp.int32)[None, :]).astype(
        jnp.bfloat16
    )
    spread = node_mask[:, :, None] * row_stats[:, None, :]
    return spread.reshape(row_stats.shape[0], node_total * row_stats.shape[1])


def bin_onehot(code_block, bin_count):
    return (code_block[:, :, None] == jnp.arange(bin_count, dtype=jnp.int32)).astype(jnp.bfloat16)


def local(bin_codes, node_ids, margins, labels, split_feature, split_bin):
    node_total = split_feature.shape[0]
    targets = margins.shape[0]
    row_count = margins.shape[1]
    local_features = bin_codes.shape[0]
    bin_count = BINS
    owned = local_features // lax.axis_size("client")
    channels = node_total * 2 * targets
    probability = jax.nn.sigmoid(margins)
    gradient = (probability - labels).astype(jnp.bfloat16)
    hessian = (probability * (1.0 - probability)).astype(jnp.bfloat16)
    row_stats = jnp.concatenate([gradient, hessian], axis=0).T
    expanded = expand(row_stats, node_ids, node_total)
    group_size = math.gcd(lax.axis_size("client") * owned, 8)
    selected = bin_codes
    selected = selected.reshape(
        lax.axis_size("client") * owned // group_size, group_size, row_count
    )

    def one_group(running, feature_group):
        result = jnp.einsum(
            "frb,rc->fbc",
            bin_onehot(feature_group, bin_count),
            expanded,
            preferred_element_type=jnp.float32,
        )
        return (running, result)

    unused, groups = lax.scan(one_group, None, selected)
    histogram = lax.psum_scatter(
        groups.reshape(lax.axis_size("client") * owned, bin_count, channels),
        "client",
        scatter_dimension=0,
        tiled=True,
    )
    prefix = jnp.cumsum(histogram, axis=1).reshape(owned, bin_count, node_total, 2 * targets)
    split_gains = gain_table(prefix, targets).transpose(2, 0, 1)
    first_global = lax.axis_index("feat") * local_features + lax.axis_index("client") * owned
    feature_mask = (
        jnp.arange(owned, dtype=jnp.int32)[None, :] + first_global == split_feature[:, None]
    ).astype(jnp.float32)
    bin_mask = (jnp.arange(bin_count, dtype=jnp.int32)[None, :] == split_bin[:, None]).astype(
        jnp.float32
    )
    picked = jnp.einsum(
        "nf,nb,fbnk->nk", feature_mask, bin_mask, prefix, precision=lax.Precision.HIGHEST
    )
    totals = jnp.einsum("nf,fnk->nk", feature_mask, prefix[:, -1], precision=lax.Precision.HIGHEST)
    left_sums, node_sums = lax.psum((picked, totals), ("client", "feat"))
    leaf_weights = leaf_table(left_sums, node_sums, targets)
    node_mask = (node_ids[:, None] == jnp.arange(node_total, dtype=jnp.int32)[None, :]).astype(
        jnp.int32
    )
    slab_owner = (split_feature // local_features == lax.axis_index("feat")).astype(jnp.int32)
    slab_column = split_feature % local_features
    row_owner = jnp.sum(node_mask * slab_owner[None, :], axis=1)
    row_column = jnp.sum(node_mask * slab_column[None, :], axis=1)
    row_bin = jnp.sum(node_mask * split_bin[None, :], axis=1)
    row_code = jnp.take_along_axis(bin_codes, row_column[None, :], axis=0)[0]
    local_side = row_owner * (row_code > row_bin).astype(jnp.int32)
    right_side = lax.psum(local_side, "feat")
    child = 2 * node_ids + right_side
    child_mask = (jnp.arange(2 * node_total, dtype=jnp.int32)[:, None] == child[None, :]).astype(
        jnp.float32
    )
    lookup = jnp.dot(leaf_weights.T, child_mask, precision=lax.Precision.HIGHEST)
    new_margins = margins + step_eta * lookup
    return (split_gains, leaf_weights, new_margins)


def solution(mesh):
    in_specs = (P("feat", "client"), P("client"), P(None, "client"), P(None, "client"), P(), P())
    out_specs = (P(None, ("feat", "client"), None), P(), P(None, "client"))
    return jax.shard_map(local, mesh=mesh, in_specs=in_specs, out_specs=out_specs, check_vma=False)
```

profile of v0, /device:TPU:1, one launch (start us, length us, event | category | flops | bytes accessed | tf_op | source)
XLA Modules:
  0.0 383.9 jit_solution(3577392374156477702)
XLA Ops:
  7.2 0.7 fusion.12
  7.9 1.0 subtract_convert_fusion
  8.9 37.1 %while.11 = (s32[]{:T(128)}, f32[8,8,256,256]{3,2,1,0:T(8,128)}, s32[8,8,1536]{2,1,0:T(8,128)}, bf16[1536,32]{0,1:T(8,128)(2,1)S(1)}, bf16[1536,8]{0,1:T(8,128)(2,1)S(1)}, /*index=5*/s32[]{:T(128)}) while((s32[]{:T(128)}, f32[8,8,256,256]{3,2,1,0:T(8,128)}, s32[8,8,1536]{2,1,0:T(8,128)}, bf16[1536,32]{0,1:T(8,128)(2,1)S(1)}, ...), condition=%wide.region_1.2_spmd.clone, body=%wide.region_0.1_spmd.clone.sunk | while | flops 1614151680 | bytes 3940937 | solution.py:76
  8.9 0.8 dynamic-slice_bitcast_fusion.2
  9.8 3.8 bitcast_dynamic-update-slice_fusion.2
  13.6 0.8 dynamic-slice_bitcast_fusion.2
  14.5 3.7 bitcast_dynamic-update-slice_fusion.2
  18.2 0.8 dynamic-slice_bitcast_fusion.2
  19.1 3.8 bitcast_dynamic-update-slice_fusion.2
  22.8 0.8 dynamic-slice_bitcast_fusion.2
  23.7 3.8 bitcast_dynamic-update-slice_fusion.2
  27.5 0.8 dynamic-slice_bitcast_fusion.2
  28.3 3.8 bitcast_dynamic-update-slice_fusion.2
  32.2 0.8 dynamic-slice_bitcast_fusion.2
  33.0 3.7 bitcast_dynamic-update-slice_fusion.2
  36.8 0.8 dynamic-slice_bitcast_fusion.2
  37.6 3.8 bitcast_dynamic-update-slice_fusion.2
  41.4 0.8 dynamic-slice_bitcast_fusion.2
  42.3 3.8 bitcast_dynamic-update-slice_fusion.2
  46.1 0.6 copy-done.5
  47.1 12.7 %gather_fusion = s32[1536]{0:T(1024)S(1)} fusion(s32[64,1536]{1,0:T(8,128)S(1)} %bitcast.56, s32[1536]{0:T(1024)S(1)} %fusion.24), kind=kCustom, calls=%fused_computation | custom fusion | bytes 24576 | tf_op jit(solution)/shard_map/jit(take_along_axis)/gather | solution.py:106
  59.8 9.3 %psum.23 = s32[1536]{0:T(1024)S(1)} all-reduce(s32[1536]{0:T(1024)S(1)} %fusion.20), channel_id=1, replica_groups=mesh['client'=32,'feat'=8] {'feat'}, use_global_device_ids=true, to_apply=%region_11.12 | all-reduce | flops 1536 | bytes 12288 | tf_op jit(solution)/shard_map/psum | solution.py:108
  69.3 223.3 %reduce-scatter.2.cloned.1.call-done = f32[2,256,256]{2,1,0:T(8,128)} async-done(((f32[64,256,256]{2,1,0:T(8,128)}), f32[2,256,256]{2,1,0:T(8,128)}) %reduce-scatter.2.cloned.1.call-update) | async-done | bytes 524304 | tf_op jit(solution)/shard_map/reduce_scatter | solution.py:77
  292.6 1.5 fusion.7
  294.1 0.2 broadcast_add_fusion
  294.3 0.2 copy.26
  294.7 0.3 slice_reduce_fusion.1
  295.1 0.6 fusion.5
  296.1 79.1 %all-reduce = (f32[8,32]{1,0:T(8,128)S(1)}, f32[8,32]{1,0:T(8,128)S(1)}) all-reduce(f32[8,32]{1,0:T(8,128)S(1)} %bitcast.68, f32[8,32]{1,0:T(8,128)S(1)} %bitcast.69), channel_id=1, replica_groups=mesh['client'=32,'feat'=8] {'client','feat'}, use_global_device_ids=true, to_apply=%region_7.8 | all-reduce | flops 512 | bytes 4096 | tf_op jit(solution)/shard_map/psum | solution.py:96
  375.3 0.2 subtract_reduce_fusion
  375.5 0.6 copy.28
  376.1 0.9 fusion.4
  (47 shorter events, 1.8 us)
Async XLA Ops:
  7.2 285.4 %reduce-scatter.2.cloned.1.call-start = ((), (), s32[]{:S(2)}) async-start(), calls=%async_computation.1 | async-start | bytes 17301504 | tf_op jit(solution)/shard_map/reduce_scatter | solution.py:77
  46.1 0.7 copy-start.5
  46.1 0.7 copy-start.2
  46.1 0.7 copy-start.4
  46.1 1.0 copy-start
  46.1 330.1 %copy-start.1 = (f32[16,1536]{1,0:T(8,128)S(1)}, f32[16,1536]{1,0:T(8,128)}, u32[]{:S(2)}) copy-start(f32[16,1536]{1,0:T(8,128)} %param.10) | copy-start | bytes 294916
  375.3 1.7 copy-start.3
Sparse Core Ops, SparseCore 0:
  46.2 246.3 reduce-scatter.1
where the time goes:
time: 385 us; the launch traced here: 384 us
  waiting for transfers between devices  223 us (58%)
  blocking collectives  88.4 us (23%)
  matrix products  32 us (8%)
  local copies, waits for them, and re-layouts  21.1 us (5%)
  between operations  14.2 us (4%)
  other arithmetic  4.78 us (1%)
    reduce_scatter x1, waiting for transfers between devices, local(): lax.psum_scatter(groups.reshape(lax.axis_size('client') * owned, bin_coun...  223 us
    psum x1, blocking collectives, local(): left_sums, node_sums = lax.psum((picked, totals), ('client', 'feat'))  79.1 us
    dot_general x8, matrix products, one_group(): jnp.einsum('frb,rc->fbc', bin_onehot(feature_group, bin_count), expanded,...  30.2 us
    gather x1, local copies, waits for them, and re-layouts, local(): row_code = jnp.take_along_axis(bin_codes, row_column[None, :], axis=0)[0]  12.7 us
    psum x1, blocking collectives, local(): right_side = lax.psum(local_side, 'feat')  9.3 us
  transfers between devices with their start and end apart: 1, of which 1 were waited for; matrix products, arithmetic and copies ran while one was open for 3% of the time, Pallas kernels for 0%

commit v1 on v0

v1 whole, which is shorter than its diff:
```python
import jax
import jax.numpy as jnp
from jax import lax
from jax.experimental import pallas as pl
from jax.experimental.pallas import tpu as pltpu
from jax.sharding import PartitionSpec as P

F32 = jnp.float32
BF16 = jnp.bfloat16
MESH = pl.DeviceIdType.MESH
BINS = 256
NODES = 8
TARGETS = 16
CH = 2 * TARGETS
X, Y, Z = 4, 4, 8
CLIENTS = X * Z
FEATS = 2 * Y
ROWS = 1536
QUARTER = ROWS // Y
HALF = ROWS // 2
SLAB = 64
OWNED = 2
reg_lambda = 1.0
step_eta = 0.5
CONTRACT_LAST = (((1,), (1,)), ((), ()))


def split3(a):
    hi = a.astype(BF16)
    rest = a - hi.astype(F32)
    mid = rest.astype(BF16)
    low = (rest - mid.astype(F32)).astype(BF16)
    return hi, mid, low


def dot3(a, b):
    hi, mid, low = split3(a)
    out = jnp.dot(low, b, preferred_element_type=F32)
    out = out + jnp.dot(mid, b, preferred_element_type=F32)
    return out + jnp.dot(hi, b, preferred_element_type=F32)


def remote(src, dst, send, recv, client, feat):
    return pltpu.make_async_remote_copy(
        src_ref=src,
        dst_ref=dst,
        send_sem=send,
        recv_sem=recv,
        device_id=(client, feat),
        device_id_type=MESH,
    )


def kernel(
    split_feature,
    split_bin,
    codes,
    node_ids,
    margins,
    labels,
    gains_out,
    leaf_out,
    margins_out,
    msg,
    codes_all,
    stats,
    pieces,
    sides,
    sums,
    acc,
    ss_codes,
    rs_codes,
    ss_side,
    rs_side,
    ss_sums,
    rs_sums,
    ss_z,
    rs_z,
    ss_piece,
    rs_piece,
):
    me = lax.axis_index("client")
    feat = lax.axis_index("feat")
    x = me // Z
    z = me % Z
    y = feat // 2
    k = feat % 2
    kp = z % 2
    zz_own = z // 2

    barrier = pltpu.get_barrier_semaphore()

    def greet_client(j, carry):
        pl.semaphore_signal(
            barrier, inc=1, device_id=((me + j) % CLIENTS, feat), device_id_type=MESH
        )
        return carry

    def greet_feat(j, carry):
        pl.semaphore_signal(
            barrier, inc=1, device_id=(me, (feat + j) % FEATS), device_id_type=MESH
        )
        return carry

    lax.fori_loop(1, CLIENTS, greet_client, 0)
    lax.fori_loop(1, FEATS, greet_feat, 0)

    node = node_ids[...]

    node_f = node.astype(F32)
    node_pair = jnp.concatenate([node_f[:, :HALF], node_f[:, HALF:]], axis=0).astype(BF16)

    def fill(q, carry):
        block = codes[pl.ds(pl.multiple_of(8 * q, 8), 8), :].astype(F32)
        for i in range(4):
            pair = block[OWNED * i : OWNED * (i + 1)].astype(BF16)
            msg[4 * q + i, 0] = pair[:, :HALF]
            msg[4 * q + i, 1] = pair[:, HALF:]
            msg[4 * q + i, 2] = node_pair
        return carry

    lax.fori_loop(0, CLIENTS // 4, fill, 0)

    probability = 1.0 / (1.0 + jnp.exp(-margins[...]))
    stats[0:TARGETS, :] = (probability - labels[...]).astype(BF16)
    stats[TARGETS:CH, :] = (probability * (1.0 - probability)).astype(BF16)

    side = jnp.zeros((1, ROWS), F32)
    for n in range(NODES):
        column = split_feature[n] - feat * SLAB
        held = jnp.where((column >= 0) & (column < SLAB), 1.0, 0.0)
        row = codes[pl.ds(jnp.clip(column, 0, SLAB - 1), 1), :]
        right = jnp.where((row > split_bin[n]) & (node == n), 1.0, 0.0)
        side = side + held * right
    sides[feat] = jnp.concatenate([side[:, :HALF], side[:, HALF:]], axis=0).astype(BF16)

    def piece_at(ra, rb, par):
        ax = ra * (1 - par) + rb * par
        ay = ra * par + rb * (1 - par)
        px = (x + ax) % X
        quarter = (y + ay) % Y
        return px, quarter, (quarter * X + px) * 2 + par

    first = piece_at(0, 0, k)[2]

    @pl.when(k == kp)
    def _():
        pieces[first, zz_own] = stats[:, pl.ds(pl.multiple_of(y * QUARTER, 128), QUARTER)]

    pl.semaphore_wait(barrier, CLIENTS - 1 + FEATS - 1)

    def z_copy(j):
        to = (z + j) % Z
        return remote(
            pieces.at[first, zz_own],
            pieces.at[first, zz_own],
            ss_z.at[to],
            rs_z.at[zz_own],
            x * Z + to,
            feat,
        )

    @pl.when(k == kp)
    def _():
        for j in (4, 3, 5, 2, 6, 1, 7):
            z_copy(j).start()

    def side_copy(j):
        to = (feat + j) % FEATS
        return remote(sides.at[feat], sides.at[feat], ss_side.at[to], rs_side.at[feat], me, to)

    for j in range(1, FEATS):
        side_copy(j).start()

    def codes_copy(j):
        to = (me + j) % CLIENTS
        return remote(msg.at[to], codes_all.at[me], ss_codes.at[to], rs_codes.at[me], to, feat)

    def send_codes(j, carry):
        codes_copy(j).start()
        return carry

    lax.fori_loop(1, CLIENTS, send_codes, 0)
    own_codes = pltpu.make_async_copy(msg.at[me], codes_all.at[me], rs_codes.at[me])
    own_codes.start()

    for j in range(1, FEATS):
        frm = (feat + j) % FEATS
        remote(sides.at[frm], sides.at[frm], ss_side.at[frm], rs_side.at[frm], me, frm).wait_recv()
    side_pair = sides[0].astype(F32)
    for j in range(1, FEATS):
        side_pair = side_pair + sides[j].astype(F32)
    side = jnp.concatenate([side_pair[0:1], side_pair[1:2]], axis=1)
    child = 2 * node + side.astype(jnp.int32)
    node_iota = lax.broadcasted_iota(jnp.int32, (NODES, ROWS), 0)
    left_mask = jnp.where(2 * node_iota == child, 1.0, 0.0)
    node_mask = jnp.where(node_iota == node, 1.0, 0.0)
    mask = jnp.concatenate([left_mask, node_mask], axis=0).astype(BF16)
    part = lax.dot_general(mask, stats[...], CONTRACT_LAST, preferred_element_type=F32)
    sums[me] = jnp.concatenate(
        [part[:NODES], part[NODES:], jnp.zeros((NODES, 128 - 2 * CH), F32)], axis=1
    )

    def sums_copy(j):
        to = (me + j) % CLIENTS
        return remote(sums.at[me], sums.at[me], ss_sums.at[to], rs_sums.at[me], to, feat)

    def send_sums(j, carry):
        sums_copy(j).start()
        return carry

    lax.fori_loop(1, CLIENTS, send_sums, 0)

    def order(t):
        late = (t + 12) // 16
        last = (t + 4) // 16
        j = (1 - late) * t + late * (1 - last) * ((t - 4) // 2) + last * (t - 12)
        ra = j + j // 2 - 2 * (j // 3)
        rb = late * (1 - last) * (3 - 2 * (t % 2)) + 2 * last
        return ra, rb

    def along(da, db):
        ax = da * (1 - k) + db * k
        ay = da * k + db * (1 - k)
        return ((x + ax) % X) * Z + z, ((y + ay) % Y) * 2 + k

    def piece_copy(p, t, slot, client, to_feat):
        return remote(
            pieces.at[p], pieces.at[p], ss_piece.at[t * 5 + slot], rs_piece.at[p], client, to_feat
        )

    def piece_sends(t, act):
        ra, rb = order(t)
        p = piece_at(ra, rb, k)[2]
        act(piece_copy(p, t, 4, me, y * 2 + (1 - k)))

        @pl.when((rb == 0) & (ra == 0))
        def _():
            for slot, d in ((0, 1), (1, 3)):
                act(piece_copy(p, t, slot, *along(d, 0)))

        @pl.when((rb == 0) & (ra == 1))
        def _():
            act(piece_copy(p, t, 1, *along(3, 0)))

        @pl.when(rb == 0)
        def _():
            for slot, d in ((2, 1), (3, 3)):
                act(piece_copy(p, t, slot, *along(0, d)))

        @pl.when((rb == 3) & ((ra == 0) | (ra == 3)))
        def _():
            act(piece_copy(p, t, 2, *along(0, 1)))

        @pl.when((rb == 1) & ((ra == 1) | (ra == 2)))
        def _():
            act(piece_copy(p, t, 3, *along(0, 3)))

    def wait_piece(p):
        remote(
            pieces.at[p], pieces.at[p], ss_piece.at[0], rs_piece.at[p], me, y * 2 + (1 - k)
        ).wait_recv()

    def start(copy):
        copy.start()

    def wait_send(copy):
        copy.wait_send()

    for j in range(4):

        @pl.when(2 * j + k != z)
        def _():
            remote(
                pieces.at[first, j],
                pieces.at[first, j],
                ss_z.at[2 * j + k],
                rs_z.at[j],
                x * Z + 2 * j + k,
                feat,
            ).wait_recv()

    piece_sends(0, start)

    acc[...] = jnp.zeros_like(acc)

    def wait_codes(px, par):
        for j in range(4):
            frm = px * Z + 2 * j + par
            pltpu.make_async_copy(msg.at[frm], codes_all.at[frm], rs_codes.at[frm]).wait()

    def step(t, carry):
        @pl.when(t < 15)
        def _():
            ra, rb = order(t + 1)
            wait_piece(piece_at(ra, rb, k)[2])
            piece_sends(t + 1, start)

        ra, rb = order(t)
        code_list = []
        node_list = []
        stat_list = []
        for which in range(2):
            par = k * (1 - which) + (1 - k) * which
            px, quarter, p = piece_at(ra, rb, par)

            @pl.when(((1 - par) * rb + par * ra) == 0)
            def _():
                wait_codes(px, par)

            if which == 1:
                wait_piece(p)
            half = quarter // 2
            lanes = pl.ds(pl.multiple_of((quarter % 2) * QUARTER, 128), QUARTER)
            for j in range(4):
                frm = px * Z + 2 * j + par
                code_list.append(codes_all[frm, half, :, lanes].astype(F32))
                pair = codes_all[frm, 2, :, lanes].astype(F32)
                node_list.append(jnp.where(half == 0, pair[0:1], pair[1:2]))
                stat_list.append(pieces[p, j])
        code = jnp.concatenate(code_list, axis=1).astype(jnp.int32)
        nodes = jnp.concatenate(node_list, axis=1).astype(jnp.int32)
        stat = jnp.concatenate(stat_list, axis=1).astype(F32)
        width = code.shape[1]
        bin_iota = lax.broadcasted_iota(jnp.int32, (BINS, width), 0)
        onehot = jnp.concatenate(
            [jnp.where(code[f : f + 1] == bin_iota, 1.0, 0.0).astype(BF16) for f in range(OWNED)],
            axis=0,
        )
        spread = jnp.concatenate(
            [jnp.where(nodes == n, stat, 0.0).astype(BF16) for n in range(NODES)], axis=0
        )
        acc[...] += lax.dot_general(spread, onehot, CONTRACT_LAST, preferred_element_type=F32)
        return carry

    lax.fori_loop(0, 16, step, 0)

    def wait_sums(j, carry):
        frm = (me + j) % CLIENTS
        remote(sums.at[frm], sums.at[frm], ss_sums.at[frm], rs_sums.at[frm], frm, feat).wait_recv()
        return carry

    lax.fori_loop(1, CLIENTS, wait_sums, 0)
    total = jnp.sum(sums[...], axis=0)
    left = total[:, :CH]
    whole = total[:, CH : 2 * CH]
    right = whole - left
    left_weight = -left[:, :TARGETS] / (left[:, TARGETS:] + reg_lambda)
    right_weight = -right[:, :TARGETS] / (right[:, TARGETS:] + reg_lambda)
    rows = []
    for n in range(NODES):
        rows.append(left_weight[n : n + 1])
        rows.append(right_weight[n : n + 1])
    weights = jnp.concatenate(rows, axis=0)
    leaf_out[...] = weights
    columns = jnp.concatenate([weights, jnp.zeros((2 * NODES, 128 - TARGETS), F32)], axis=1).T
    child_iota = lax.broadcasted_iota(jnp.int32, (2 * NODES, ROWS), 0)
    child_mask = jnp.where(child_iota == child, 1.0, 0.0).astype(BF16)
    lookup = dot3(columns[:TARGETS, :], child_mask)
    margins_out[...] = margins[...] + step_eta * lookup

    row_bin = lax.broadcasted_iota(jnp.int32, (BINS, BINS), 0)
    col_bin = lax.broadcasted_iota(jnp.int32, (BINS, BINS), 1)
    upto = jnp.where(row_bin <= col_bin, 1.0, 0.0).astype(BF16)
    for f in range(OWNED):
        prefix = dot3(acc[:, f * BINS : (f + 1) * BINS], upto)
        for n in range(NODES):
            gl = prefix[n * CH : n * CH + TARGETS]
            hl = prefix[n * CH + TARGETS : (n + 1) * CH]
            g = gl[:, BINS - 1 :]
            h = hl[:, BINS - 1 :]
            value = gl * gl / (hl + reg_lambda)
            value = value + (g - gl) * (g - gl) / (h - hl + reg_lambda)
            value = value - g * g / (h + reg_lambda)
            gains_out[n, f : f + 1, :] = 0.5 * jnp.sum(value, axis=0, keepdims=True)

    @pl.when(k == kp)
    def _():
        for j in range(1, Z):
            z_copy(j).wait_send()

    for j in range(1, FEATS):
        side_copy(j).wait_send()

    def end_client(j, carry):
        codes_copy(j).wait_send()
        sums_copy(j).wait_send()
        return carry

    lax.fori_loop(1, CLIENTS, end_client, 0)

    def end_piece(t, carry):
        piece_sends(t, wait_send)
        return carry

    lax.fori_loop(0, 16, end_piece, 0)


def local(bin_codes, node_ids, margins, labels, split_feature, split_bin):
    vmem = pl.BlockSpec(memory_space=pltpu.VMEM)
    smem = pl.BlockSpec(memory_space=pltpu.SMEM)
    dma = pltpu.SemaphoreType.DMA
    return pl.pallas_call(
        kernel,
        out_shape=(
            jax.ShapeDtypeStruct((NODES, OWNED, BINS), F32),
            jax.ShapeDtypeStruct((2 * NODES, TARGETS), F32),
            jax.ShapeDtypeStruct((TARGETS, ROWS), F32),
        ),
        in_specs=[smem, smem, vmem, vmem, vmem, vmem],
        out_specs=(vmem, vmem, vmem),
        scratch_shapes=[
            pltpu.VMEM((CLIENTS, 3, 2, HALF), BF16),
            pltpu.VMEM((CLIENTS, 3, 2, HALF), BF16),
            pltpu.VMEM((CH, ROWS), BF16),
            pltpu.VMEM((2 * X * Y, 4, CH, QUARTER), BF16),
            pltpu.VMEM((FEATS, 2, HALF), BF16),
            pltpu.VMEM((CLIENTS, NODES, 128), F32),
            pltpu.VMEM((NODES * CH, OWNED * BINS), F32),
            dma((CLIENTS,)),
            dma((CLIENTS,)),
            dma((FEATS,)),
            dma((FEATS,)),
            dma((CLIENTS,)),
            dma((CLIENTS,)),
            dma((Z,)),
            dma((4,)),
            dma((80,)),
            dma((2 * X * Y,)),
        ],
        compiler_params=pltpu.CompilerParams(
            collective_id=0, has_side_effects=True, vmem_limit_bytes=60 << 20
        ),
        name="level",
    )(split_feature, split_bin, bin_codes, node_ids.reshape(1, ROWS), margins, labels)


def solution(mesh):
    in_specs = (P("feat", "client"), P("client"), P(None, "client"), P(None, "client"), P(), P())
    out_specs = (P(None, ("feat", "client"), None), P(), P(None, "client"))
    return jax.shard_map(local, mesh=mesh, in_specs=in_specs, out_specs=out_specs, check_vma=False)
```

time: 385 us -> 55.6 us (0.14)
  waiting for transfers between devices: 223 us -> 0 us
  blocking collectives: 88.4 us -> 0 us
  Pallas kernels: 0 us -> 50 us
  matrix products: 32 us -> 0 us
  local copies, waits for them, and re-layouts: 21.1 us -> 4.77 us
  between operations: 14.2 us -> 0.65 us
  other arithmetic: 4.78 us -> 0 us
    reduce_scatter x1 -> x0, waiting for transfers between devices: 223 us -> none  [local(): lax.psum_scatter(groups.reshape(lax.axis_size('client') * owned, bin_coun...]
    psum x2 -> x0, blocking collectives: 88.4 us -> none  [the longest x1 79.1 us: local(): left_sums, node_sums = lax.psum((picked, totals), ('client', 'feat'))]
    pallas_call x0 -> x1, Pallas kernels: none -> 50 us  [local(): pl.pallas_call(kernel, out_shape=(jax.ShapeDtypeStruct((NODES, OWNED, BIN...]
    dot_general x12 -> x0, matrix products: 32 us -> none  [the longest x8 30.2 us: one_group(): jnp.einsum('frb,rc->fbc', bin_onehot(feature_group, bin_count), expanded,...]
    gather x1 -> x0, local copies, waits for them, and re-layouts: 12.7 us -> none  [local(): row_code = jnp.take_along_axis(bin_codes, row_column[None, :], axis=0)[0]]
    eq x8 -> x0, local copies, waits for them, and re-layouts: 6.42 us -> none  [bin_onehot(): code_block[:, :, None] == jnp.arange(bin_count, dtype=jnp.int32)]
  transfers between devices with their start and end apart: 1 -> 0, of which waited for: 1 -> 0; matrix products, arithmetic and copies ran while one was open for 3% -> 0% of each run, Pallas kernels for 0% -> 0%
where the time goes in v1:
time: 55.6 us; the launch traced here: 55.4 us
  Pallas kernels  50 us (90%)
  local copies, waits for them, and re-layouts  4.77 us (9%)
  between operations  0.65 us (1%)
    pallas_call x1, Pallas kernels, local(): pl.pallas_call(kernel, out_shape=(jax.ShapeDtypeStruct((NODES, OWNED, BIN...  50 us
    unnamed x5, local copies, waits for them, and re-layouts  3.47 us
    reshape x1, local copies, waits for them, and re-layouts, local(): node_ids.reshape(1, ROWS)  1.3 us

profile of v1, /device:TPU:1, one launch (start us, length us, event | category | flops | bytes accessed | tf_op | source)
XLA Modules:
  0.0 55.4 jit_solution(8168955715051222550)
XLA Ops:
  0.6 1.3 %reshape.9.node_ids = s32[1,1536]{1,0:T(1,128)} reshape(s32[1536]{0:T(1024)} %param.7) | data formatting | bytes 12288 | tf_op jit(solution)/shard_map/reshape | solution.py:435
  1.9 50.0 %level.1 = (f32[8,2,256]{2,1,0:T(2,128)}, f32[16,16]{1,0:T(8,128)}, f32[16,1536]{1,0:T(8,128)}) custom-call(s32[8]{0:T(128)} %split_feature.1, s32[8]{0:T(128)} %split_bin.1, s32[64,1536]{1,0:T(8,128)} %codes.1, s32[1,1536]{1,0:T(1,128)} %reshape.9.node_ids, f32[16,1536]{1,0:T(8,128)} %margins.1, f32[16,1536]{1,0:T(8,128)} %labels.1), custom_call_target="tpu_custom_call" | custom-call | tf_op jit(solution)/shard_map/level/pallas_call | solution.py:403
  51.9 0.0 copy-start
  51.9 1.3 %copy.12 = f32[8,2,256]{2,1,0:T(2,128)} copy(f32[8,2,256]{2,1,0:T(2,128)} %get-tuple-element.6) | data formatting | bytes 32768
  53.2 0.0 copy-done
  53.2 0.6 %copy.13 = f32[16,16]{1,0:T(8,128)} copy(f32[16,16]{1,0:T(8,128)S(1)} %copy-done) | data formatting | bytes 2048
  53.8 1.5 %copy.14 = f32[16,1536]{1,0:T(8,128)} copy(f32[16,1536]{1,0:T(8,128)} %get-tuple-element.8) | data formatting | bytes 196608
Async XLA Ops:
  51.9 1.3 %copy-start = (f32[16,16]{1,0:T(8,128)S(1)}, f32[16,16]{1,0:T(8,128)}, u32[]{:S(2)}) copy-start(f32[16,16]{1,0:T(8,128)} %get-tuple-element.7) | copy-start | bytes 3076

commit v2 on v1

v2 whole, which is shorter than its diff:
```python
import jax
import jax.numpy as jnp
from jax import lax
from jax.experimental import pallas as pl
from jax.experimental.pallas import tpu as pltpu
from jax.sharding import PartitionSpec as P

F32 = jnp.float32
BF16 = jnp.bfloat16
MESH = pl.DeviceIdType.MESH
BINS = 256
NODES = 8
TARGETS = 16
CH = 2 * TARGETS
X, Y, Z = 4, 4, 8
CLIENTS = X * Z
FEATS = 2 * Y
ROWS = 1536
QUARTER = ROWS // Y
HALF = ROWS // 2
SLAB = 64
OWNED = 2
reg_lambda = 1.0
step_eta = 0.5
ORDER = (
    (0, 0), (1, 0), (3, 0), (0, 1), (0, 3), (1, 1), (3, 3), (1, 3), (3, 1),
    (2, 0), (0, 2), (2, 1), (2, 3), (1, 2), (3, 2), (2, 2),
)
AHEAD = 2
CONTRACT_LAST = (((1,), (1,)), ((), ()))


def split3(a):
    hi = a.astype(BF16)
    rest = a - hi.astype(F32)
    mid = rest.astype(BF16)
    low = (rest - mid.astype(F32)).astype(BF16)
    return hi, mid, low


def dot3(a, b):
    hi, mid, low = split3(a)
    out = jnp.dot(low, b, preferred_element_type=F32)
    out = out + jnp.dot(mid, b, preferred_element_type=F32)
    return out + jnp.dot(hi, b, preferred_element_type=F32)


def remote(src, dst, send, recv, client, feat):
    return pltpu.make_async_remote_copy(
        src_ref=src,
        dst_ref=dst,
        send_sem=send,
        recv_sem=recv,
        device_id=(client, feat),
        device_id_type=MESH,
    )


def kernel(
    feature_in,
    bin_in,
    codes_in,
    node_in,
    margins_in,
    labels_in,
    gains_out,
    leaf_out,
    margins_out,
    split_feature,
    split_bin,
    codes,
    node_ids,
    margins,
    labels,
    ls,
    msg,
    codes_all,
    stats,
    pieces,
    sides,
    child_ref,
    parts,
    sums,
    node_sums,
    acc,
    far,
    ss_codes,
    rs_codes,
    ss_side,
    rs_side,
    ss_sums,
    rs_sums,
    ss_node,
    rs_node,
    ss_z,
    rs_z,
    ss_piece,
    rs_piece,
):
    me = lax.axis_index("client")
    feat = lax.axis_index("feat")
    x = lax.div(me, Z)
    z = lax.rem(me, Z)
    y = lax.div(feat, 2)
    k = lax.rem(feat, 2)
    kp = lax.rem(z, 2)
    zz_own = lax.div(z, 2)

    barrier = pltpu.get_barrier_semaphore()

    for j in (4, 3, 5, 2, 6, 1, 7):
        pl.semaphore_signal(
            barrier, inc=1, device_id=(x * Z + lax.rem(z + j, Z), feat), device_id_type=MESH
        )
    for j in (2, 1, 3):
        pl.semaphore_signal(
            barrier, inc=1, device_id=((lax.rem(x + j, X)) * Z + z, feat), device_id_type=MESH
        )
    for j in range(1, FEATS):
        pl.semaphore_signal(
            barrier, inc=1, device_id=(me, lax.rem(feat + j, FEATS)), device_id_type=MESH
        )

    loads = [
        pltpu.make_async_copy(src, dst, ls.at[i])
        for i, (src, dst) in enumerate(
            (
                (margins_in, margins),
                (labels_in, labels),
                (node_in, node_ids),
                (codes_in, codes),
                (feature_in, split_feature),
                (bin_in, split_bin),
            )
        )
    ]
    for load in loads:
        load.start()
    for load in loads:
        load.wait()

    node = jnp.concatenate([node_ids[i : i + 1, :] for i in range(ROWS // 128)], axis=1)

    node_f = node.astype(F32)
    node_pair = jnp.concatenate([node_f[:, :HALF], node_f[:, HALF:]], axis=0).astype(BF16)

    def fill(q, carry):
        block = codes[pl.ds(pl.multiple_of(8 * q, 8), 8), :].astype(F32)
        for i in range(4):
            pair = block[OWNED * i : OWNED * (i + 1)].astype(BF16)
            msg[4 * q + i, 0] = pair[:, :HALF]
            msg[4 * q + i, 1] = pair[:, HALF:]
            msg[4 * q + i, 2] = node_pair
        return carry

    lax.fori_loop(0, CLIENTS // 4, fill, 0)

    probability = 1.0 / (1.0 + jnp.exp(-margins[...]))
    stats[0:TARGETS, :] = (probability - labels[...]).astype(BF16)
    stats[TARGETS:CH, :] = (probability * (1.0 - probability)).astype(BF16)

    side = jnp.zeros((1, ROWS), F32)
    for n in range(NODES):
        column = split_feature[n] - feat * SLAB
        held = jnp.where((column >= 0) & (column < SLAB), 1.0, 0.0)
        row = codes[pl.ds(jnp.clip(column, 0, SLAB - 1), 1), :]
        right = jnp.where((row > split_bin[n]) & (node == n), 1.0, 0.0)
        side = side + held * right
    sides[feat] = jnp.concatenate([side[:, :HALF], side[:, HALF:]], axis=0).astype(BF16)

    def piece_at(ra, rb, par):
        ax = ra * (1 - par) + rb * par
        ay = ra * par + rb * (1 - par)
        px = lax.rem(x + ax, X)
        quarter = lax.rem(y + ay, Y)
        return px, quarter, (quarter * X + px) * 2 + par

    first = piece_at(0, 0, k)[2]

    @pl.when(k == kp)
    def _():
        pieces[first, zz_own] = stats[:, pl.ds(pl.multiple_of(y * QUARTER, 128), QUARTER)]

    pl.semaphore_wait(barrier, Z - 1 + X - 1 + FEATS - 1)

    def z_copy(j):
        to = lax.rem(z + j, Z)
        return remote(
            pieces.at[first, zz_own],
            pieces.at[first, zz_own],
            ss_z.at[to],
            rs_z.at[zz_own],
            x * Z + to,
            feat,
        )

    @pl.when(k == kp)
    def _():
        for j in (4, 3, 5, 2, 6, 1, 7):
            z_copy(j).start()

    def codes_copy(dx, dz):
        to = lax.rem(x + dx, X) * Z + lax.rem(z + dz, Z)
        return remote(msg.at[to], codes_all.at[me], ss_codes, rs_codes.at[me], to, feat)

    for j in (4, 3, 5, 2, 6, 1, 7):
        codes_copy(0, j).start()
    for j in range(1, Z):
        pl.semaphore_signal(
            far, inc=1, device_id=(x * Z + lax.rem(z + j, Z), feat), device_id_type=MESH
        )

    def side_copy(j):
        to = lax.rem(feat + j, FEATS)
        return remote(sides.at[feat], sides.at[feat], ss_side, rs_side, me, to)

    for j in range(1, FEATS):
        side_copy(j).start()
    own_codes = pltpu.make_async_copy(msg.at[me], codes_all.at[me], rs_codes.at[me])
    own_codes.start()
    pl.semaphore_wait(far, Z - 1)

    def send_codes(dz, carry):
        for dx in (1, 3, 2):
            codes_copy(dx, dz).start()
        return carry

    lax.fori_loop(0, Z, send_codes, 0)

    def sums_copy(j):
        to = lax.rem(me + j, CLIENTS)
        return remote(sums.at[me], sums.at[me], ss_sums, rs_sums, to, feat)

    def node_copy(j):
        to = lax.rem(feat + j, FEATS)
        return remote(node_sums.at[feat], node_sums.at[feat], ss_node, rs_node, me, to)

    def many(ref, count, send, recv):
        return remote(ref.at[pl.ds(0, count)], ref.at[pl.ds(0, count)], send, recv, me, feat)

    def client_sums():
        many(sides, FEATS - 1, ss_side, rs_side).wait_recv()
        side_pair = sides[0].astype(F32)
        for j in range(1, FEATS):
            side_pair = side_pair + sides[j].astype(F32)
        side = jnp.concatenate([side_pair[0:1], side_pair[1:2]], axis=1)
        child = 2 * node + side.astype(jnp.int32)
        child_ref[...] = child
        node_iota = lax.broadcasted_iota(jnp.int32, (NODES, ROWS), 0)
        left_mask = jnp.where(2 * node_iota == child, 1.0, 0.0)
        node_mask = jnp.where(node_iota == node, 1.0, 0.0)
        mask = jnp.concatenate([left_mask, node_mask], axis=0).astype(BF16)
        part = lax.dot_general(mask, stats[...], CONTRACT_LAST, preferred_element_type=F32)
        parts[...] = jnp.concatenate([part, jnp.zeros((2 * NODES, 128 - CH), F32)], axis=1)
        sums[me] = jnp.concatenate(
            [
                parts[pl.ds(feat, 1), :CH],
                parts[pl.ds(NODES + feat, 1), :CH],
                jnp.zeros((1, 128 - 2 * CH), F32),
            ],
            axis=1,
        )

        def send_sums(j, carry):
            sums_copy(j).start()
            return carry

        lax.fori_loop(1, CLIENTS, send_sums, 0)

    def meet_nodes():
        many(sums, CLIENTS - 1, ss_sums, rs_sums).wait_recv()
        node_sums[feat] = jnp.sum(sums[...], axis=0)
        for j in range(1, FEATS):
            node_copy(j).start()

    def order(t):
        code = 0
        for i, (ra, rb) in enumerate(ORDER):
            code = code + jnp.where(t == i, 4 * ra + rb, 0)
        return lax.div(code, 4), lax.rem(code, 4)

    def along(da, db):
        ax = da * (1 - k) + db * k
        ay = da * k + db * (1 - k)
        return (lax.rem(x + ax, X)) * Z + z, (lax.rem(y + ay, Y)) * 2 + k

    def piece_copy(p, client, to_feat):
        return remote(pieces.at[p], pieces.at[p], ss_piece, rs_piece.at[p], client, to_feat)

    def piece_sends(ra, rb):
        p = piece_at(ra, rb, k)[2]
        piece_copy(p, me, y * 2 + (1 - k)).start()

        @pl.when((rb == 0) & (ra == 0))
        def _():
            for d in (1, 3):
                piece_copy(p, *along(d, 0)).start()

        @pl.when((rb == 0) & (ra == 1))
        def _():
            piece_copy(p, *along(3, 0)).start()

        @pl.when(rb == 0)
        def _():
            for d in (1, 3):
                piece_copy(p, *along(0, d)).start()

        @pl.when((rb == 3) & ((ra == 1) | (ra == 2)))
        def _():
            piece_copy(p, *along(0, 1)).start()

        @pl.when((rb == 1) & ((ra == 0) | (ra == 3)))
        def _():
            piece_copy(p, *along(0, 3)).start()

    def wait_piece(p):
        remote(
            pieces.at[p], pieces.at[p], ss_piece, rs_piece.at[p], me, y * 2 + (1 - k)
        ).wait_recv()

    for j in range(4):

        @pl.when(2 * j + k != z)
        def _():
            remote(
                pieces.at[first, j],
                pieces.at[first, j],
                ss_z.at[2 * j + k],
                rs_z.at[j],
                x * Z + 2 * j + k,
                feat,
            ).wait_recv()

    piece_sends(0, 0)

    def event(t):
        ra, rb = order(t)
        wait_piece(piece_at(ra, rb, k)[2])
        piece_sends(ra, rb)

    acc[...] = jnp.zeros_like(acc)

    def wait_codes(px, par):
        for j in range(4):
            frm = px * Z + 2 * j + par
            pltpu.make_async_copy(msg.at[frm], codes_all.at[frm], rs_codes.at[frm]).wait()

    def compute(steps):
        code_list = []
        node_list = []
        stat_list = []
        for ra, rb in steps:
            for which in range(2):
                par = k * (1 - which) + (1 - k) * which
                px, quarter, p = piece_at(ra, rb, par)

                @pl.when(((1 - par) * rb + par * ra) == 0)
                def _():
                    wait_codes(px, par)

                if which == 1:
                    wait_piece(p)
                half = lax.div(quarter, 2)
                lanes = pl.ds(pl.multiple_of(lax.rem(quarter, 2) * QUARTER, 128), QUARTER)
                for j in range(4):
                    frm = px * Z + 2 * j + par
                    code_list.append(codes_all[frm, half, :, lanes].astype(F32))
                    pair = codes_all[frm, 2, :, lanes].astype(F32)
                    node_list.append(jnp.where(half == 0, pair[0:1], pair[1:2]))
                    stat_list.append(pieces[p, j])
        code = jnp.concatenate(code_list, axis=1).astype(jnp.int32)
        nodes = jnp.concatenate(node_list, axis=1).astype(jnp.int32)
        stat = jnp.concatenate(stat_list, axis=1).astype(F32)
        width = code.shape[1]
        bin_iota = lax.broadcasted_iota(jnp.int32, (BINS, width), 0)
        onehot = jnp.concatenate(
            [jnp.where(code[f : f + 1] == bin_iota, 1.0, 0.0).astype(BF16) for f in range(OWNED)],
            axis=0,
        )
        spread = jnp.concatenate(
            [jnp.where(nodes == n, stat, 0.0).astype(BF16) for n in range(NODES)], axis=0
        )
        acc[...] += lax.dot_general(spread, onehot, CONTRACT_LAST, preferred_element_type=F32)

    compute([(0, 0)])
    client_sums()
    event(1)
    event(2)

    def step(t, carry):
        @pl.when(t < 7)
        def _():
            event(2 * t + 1)
            event(2 * t + 2)

        @pl.when(t == 7)
        def _():
            event(15)

        @pl.when(t == 5)
        def _():
            meet_nodes()

        compute([order(2 * t - 1), order(2 * t)])
        return carry

    lax.fori_loop(1, 8, step, 0)
    compute([order(15 + 0 * k)])

    many(node_sums, FEATS - 1, ss_node, rs_node).wait_recv()
    total = jnp.concatenate([node_sums[n] for n in range(NODES)], axis=0)
    left = total[:, :CH]
    whole = total[:, CH : 2 * CH]
    right = whole - left
    left_weight = -left[:, :TARGETS] / (left[:, TARGETS:] + reg_lambda)
    right_weight = -right[:, :TARGETS] / (right[:, TARGETS:] + reg_lambda)
    rows = []
    for n in range(NODES):
        rows.append(left_weight[n : n + 1])
        rows.append(right_weight[n : n + 1])
    weights = jnp.concatenate(rows, axis=0)
    leaf_out[...] = weights
    columns = jnp.concatenate([weights, jnp.zeros((2 * NODES, 128 - TARGETS), F32)], axis=1).T
    child_iota = lax.broadcasted_iota(jnp.int32, (2 * NODES, ROWS), 0)
    child_mask = jnp.where(child_iota == child_ref[...], 1.0, 0.0).astype(BF16)
    lookup = dot3(columns[:TARGETS, :], child_mask)
    margins_out[...] = margins[...] + step_eta * lookup

    row_bin = lax.broadcasted_iota(jnp.int32, (BINS, BINS), 0)
    col_bin = lax.broadcasted_iota(jnp.int32, (BINS, BINS), 1)
    upto = jnp.where(row_bin <= col_bin, 1.0, 0.0).astype(BF16)
    for f in range(OWNED):
        prefix = dot3(acc[:, f * BINS : (f + 1) * BINS], upto)
        for n in range(NODES):
            gl = prefix[n * CH : n * CH + TARGETS]
            hl = prefix[n * CH + TARGETS : (n + 1) * CH]
            g = gl[:, BINS - 1 :]
            h = hl[:, BINS - 1 :]
            value = gl * gl / (hl + reg_lambda)
            value = value + (g - gl) * (g - gl) / (h - hl + reg_lambda)
            value = value - g * g / (h + reg_lambda)
            gains_out[n, f : f + 1, :] = 0.5 * jnp.sum(value, axis=0, keepdims=True)

    @pl.when(k == kp)
    def _():
        for j in range(1, Z):
            z_copy(j).wait_send()

    many(sides, FEATS - 1, ss_side, rs_side).wait_send()
    many(node_sums, FEATS - 1, ss_node, rs_node).wait_send()
    many(sums, CLIENTS - 1, ss_sums, rs_sums).wait_send()
    many(msg, CLIENTS - 1, ss_codes, rs_codes.at[0]).wait_send()
    many(pieces, 2 * X * Y - 1, ss_piece, rs_piece.at[0]).wait_send()


def local(bin_codes, node_ids, margins, labels, split_feature, split_bin):
    vmem = pl.BlockSpec(memory_space=pltpu.VMEM)
    hbm = pl.BlockSpec(memory_space=pltpu.HBM)
    dma = pltpu.SemaphoreType.DMA
    return pl.pallas_call(
        kernel,
        out_shape=(
            jax.ShapeDtypeStruct((NODES, OWNED, BINS), F32),
            jax.ShapeDtypeStruct((2 * NODES, TARGETS), F32),
            jax.ShapeDtypeStruct((TARGETS, ROWS), F32),
        ),
        in_specs=[hbm] * 6,
        out_specs=(vmem, vmem, vmem),
        scratch_shapes=[
            pltpu.SMEM((NODES,), jnp.int32),
            pltpu.SMEM((NODES,), jnp.int32),
            pltpu.VMEM((SLAB, ROWS), jnp.int32),
            pltpu.VMEM((ROWS // 128, 128), jnp.int32),
            pltpu.VMEM((TARGETS, ROWS), F32),
            pltpu.VMEM((TARGETS, ROWS), F32),
            dma((6,)),
            pltpu.VMEM((CLIENTS, 3, 2, HALF), BF16),
            pltpu.VMEM((CLIENTS, 3, 2, HALF), BF16),
            pltpu.VMEM((CH, ROWS), BF16),
            pltpu.VMEM((2 * X * Y, 4, CH, QUARTER), BF16),
            pltpu.VMEM((FEATS, 2, HALF), BF16),
            pltpu.VMEM((1, ROWS), jnp.int32),
            pltpu.VMEM((2 * NODES, 128), F32),
            pltpu.VMEM((CLIENTS, 1, 128), F32),
            pltpu.VMEM((FEATS, 1, 128), F32),
            pltpu.VMEM((NODES * CH, OWNED * BINS), F32),
            pltpu.SemaphoreType.REGULAR,
            dma,
            dma((CLIENTS,)),
            dma,
            dma,
            dma,
            dma,
            dma,
            dma,
            dma((Z,)),
            dma((4,)),
            dma,
            dma((2 * X * Y,)),
        ],
        compiler_params=pltpu.CompilerParams(
            collective_id=0, has_side_effects=True, vmem_limit_bytes=36 << 20
        ),
        name="level",
    )(*[pltpu.with_memory_space_constraint(a, pltpu.HBM) for a in (split_feature, split_bin, bin_codes, node_ids.reshape(ROWS // 128, 128), margins, labels)])


def solution(mesh):
    in_specs = (P("feat", "client"), P("client"), P(None, "client"), P(None, "client"), P(), P())
    out_specs = (P(None, ("feat", "client"), None), P(), P(None, "client"))
    return jax.shard_map(local, mesh=mesh, in_specs=in_specs, out_specs=out_specs, check_vma=False)
```

time: 55.6 us -> 45.5 us (0.82)
  Pallas kernels: 50 us -> 42.9 us
  local copies, waits for them, and re-layouts: 4.77 us -> 1.85 us
    pallas_call x1, Pallas kernels: 50 us -> 42.9 us  [local(): pl.pallas_call(kernel, out_shape=(jax.ShapeDtypeStruct((NODES, OWNED, BIN...]
    unnamed x5 -> x3, local copies, waits for them, and re-layouts: 3.47 us -> 1.85 us
    reshape x1 -> x0, local copies, waits for them, and re-layouts: 1.3 us -> none  [local(): node_ids.reshape(1, ROWS)]
where the time goes in v2:
time: 45.5 us; the launch traced here: 45.4 us
  Pallas kernels  42.9 us (94%)
  local copies, waits for them, and re-layouts  1.85 us (4%)
  between operations  0.64 us (1%)
    pallas_call x1, Pallas kernels, local(): pl.pallas_call(kernel, out_shape=(jax.ShapeDtypeStruct((NODES, OWNED, BIN...  42.9 us
    unnamed x3, local copies, waits for them, and re-layouts  1.85 us

profile of v2, /device:TPU:1, one launch (start us, length us, event | category | flops | bytes accessed | tf_op | source)
XLA Modules:
  0.0 45.4 jit_solution(10632851445421427110)
XLA Ops:
  0.6 42.9 %level.1 = (f32[8,2,256]{2,1,0:T(2,128)S(1)}, f32[16,16]{1,0:T(8,128)S(1)}, f32[16,1536]{1,0:T(8,128)S(1)}) custom-call(s32[8]{0:T(128)} %feature_in.1, s32[8]{0:T(128)} %bin_in.1, s32[64,1536]{1,0:T(8,128)} %codes_in.1, s32[12,128]{1,0:T(8,128)} %bitcast.1, f32[16,1536]{1,0:T(8,128)} %margins_in.1, f32[16,1536]{1,0:T(8,128)} %labels_in.1), custom_call_target="tpu_custom_call" | custom-call | tf_op jit(solution)/shard_map/level/pallas_call | solution.py:460
  43.5 0.6 %copy.12 = f32[8,2,256]{2,1,0:T(2,128)} copy(f32[8,2,256]{2,1,0:T(2,128)S(1)} %get-tuple-element.6) | data formatting | bytes 32768
  44.1 0.6 %copy.13 = f32[16,16]{1,0:T(8,128)} copy(f32[16,16]{1,0:T(8,128)S(1)} %get-tuple-element.7) | data formatting | bytes 2048
  44.7 0.6 %copy.14 = f32[16,1536]{1,0:T(8,128)} copy(f32[16,1536]{1,0:T(8,128)S(1)} %get-tuple-element.8) | data formatting | bytes 196608

commit v3 on v2

--- a/solution.py
+++ b/solution.py
@@ -22,11 +22,14 @@
 OWNED = 2
 reg_lambda = 1.0
 step_eta = 0.5
-ORDER = (
-    (0, 0), (1, 0), (3, 0), (0, 1), (0, 3), (1, 1), (3, 3), (1, 3), (3, 1),
-    (2, 0), (0, 2), (2, 1), (2, 3), (1, 2), (3, 2), (2, 2),
+PLAN = (
+    ("add", 0, 0), ("sums",), ("near", 0, 1), ("near", 0, 3), ("near", 1, 0), ("near", 3, 0), ("codes",), ("add", 0, 1, 0, 3),
+    ("take", 2, 0), ("add", 1, 0, 3, 0), ("take", 1, 1),
+    ("take", 1, 3), ("take", 3, 1), ("take", 3, 3), ("take", 0, 2), ("add", 0, 2, 2, 0),
+    ("add", 1, 1, 1, 3), ("take", 2, 1), ("take", 2, 3), ("add", 3, 1, 3, 3), ("take", 1, 2),
+    ("take", 3, 2), ("meet",), ("add", 1, 2, 3, 2), ("take", 2, 2), ("add", 2, 1, 2, 3),
+    ("add", 2, 2),
 )
-AHEAD = 2
 CONTRACT_LAST = (((1,), (1,)), ((), ()))
 
 
@@ -136,43 +139,15 @@
     ]
     for load in loads:
         load.start()
-    for load in loads:
+    for load in loads[:2]:
         load.wait()
-
-    node = jnp.concatenate([node_ids[i : i + 1, :] for i in range(ROWS // 128)], axis=1)
-
-    node_f = node.astype(F32)
-    node_pair = jnp.concatenate([node_f[:, :HALF], node_f[:, HALF:]], axis=0).astype(BF16)
-
-    def fill(q, carry):
-        block = codes[pl.ds(pl.multiple_of(8 * q, 8), 8), :].astype(F32)
-        for i in range(4):
-            pair = block[OWNED * i : OWNED * (i + 1)].astype(BF16)
-            msg[4 * q + i, 0] = pair[:, :HALF]
-            msg[4 * q + i, 1] = pair[:, HALF:]
-            msg[4 * q + i, 2] = node_pair
-        return carry
-
-    lax.fori_loop(0, CLIENTS // 4, fill, 0)
-
     probability = 1.0 / (1.0 + jnp.exp(-margins[...]))
     stats[0:TARGETS, :] = (probability - labels[...]).astype(BF16)
     stats[TARGETS:CH, :] = (probability * (1.0 - probability)).astype(BF16)
 
-    side = jnp.zeros((1, ROWS), F32)
-    for n in range(NODES):
-        column = split_feature[n] - feat * SLAB
-        held = jnp.where((column >= 0) & (column < SLAB), 1.0, 0.0)
-        row = codes[pl.ds(jnp.clip(column, 0, SLAB - 1), 1), :]
-        right = jnp.where((row > split_bin[n]) & (node == n), 1.0, 0.0)
-        side = side + held * right
-    sides[feat] = jnp.concatenate([side[:, :HALF], side[:, HALF:]], axis=0).astype(BF16)
-
-    def piece_at(ra, rb, par):
-        ax = ra * (1 - par) + rb * par
-        ay = ra * par + rb * (1 - par)
-        px = lax.rem(x + ax, X)
-        quarter = lax.rem(y + ay, Y)
+    def piece_at(dx, dy, par):
+        px = lax.rem(x + dx, X)
+        quarter = lax.rem(y + dy, Y)
         return px, quarter, (quarter * X + px) * 2 + par
 
     first = piece_at(0, 0, k)[2]
@@ -199,6 +174,33 @@
         for j in (4, 3, 5, 2, 6, 1, 7):
             z_copy(j).start()
 
+    for load in loads[2:]:
+        load.wait()
+    node = jnp.concatenate([node_ids[i : i + 1, :] for i in range(ROWS // 128)], axis=1)
+
+    node_f = node.astype(F32)
+    node_pair = jnp.concatenate([node_f[:, :HALF], node_f[:, HALF:]], axis=0).astype(BF16)
+
+    def fill(q, carry):
+        block = codes[pl.ds(pl.multiple_of(8 * q, 8), 8), :].astype(F32)
+        for i in range(4):
+            pair = block[OWNED * i : OWNED * (i + 1)].astype(BF16)
+            msg[4 * q + i, 0] = pair[:, :HALF]
+            msg[4 * q + i, 1] = pair[:, HALF:]
+            msg[4 * q + i, 2] = node_pair
+        return carry
+
+    lax.fori_loop(0, CLIENTS // 4, fill, 0)
+
+    side = jnp.zeros((1, ROWS), F32)
+    for n in range(NODES):
+        column = split_feature[n] - feat * SLAB
+        held = jnp.where((column >= 0) & (column < SLAB), 1.0, 0.0)
+        row = codes[pl.ds(jnp.clip(column, 0, SLAB - 1), 1), :]
+        right = jnp.where((row > split_bin[n]) & (node == n), 1.0, 0.0)
+        side = side + held * right
+    sides[feat] = jnp.concatenate([side[:, :HALF], side[:, HALF:]], axis=0).astype(BF16)
+
     def codes_copy(dx, dz):
         to = lax.rem(x + dx, X) * Z + lax.rem(z + dz, Z)
         return remote(msg.at[to], codes_all.at[me], ss_codes, rs_codes.at[me], to, feat)
@@ -218,14 +220,56 @@
         side_copy(j).start()
     own_codes = pltpu.make_async_copy(msg.at[me], codes_all.at[me], rs_codes.at[me])
     own_codes.start()
+    def along(da, db):
+        ax = da * (1 - k) + db * k
+        ay = da * k + db * (1 - k)
+        return (lax.rem(x + ax, X)) * Z + z, (lax.rem(y + ay, Y)) * 2 + k
+
+    def piece_copy(p, client, to_feat):
+        return remote(pieces.at[p], pieces.at[p], ss_piece, rs_piece.at[p], client, to_feat)
+
+    def own_piece(ra, rb):
+        return piece_at(ra * (1 - k) + rb * k, ra * k + rb * (1 - k), k)[2]
+
+    def piece_sends(ra, rb):
+        p = own_piece(ra, rb)
+        to = []
+        if rb == 0 and ra == 0:
+            to += [(1, 0), (3, 0), (2, 0)]
+        if rb == 0:
+            to += [(0, 1), (0, 3)]
+        if rb == 3 and ra in (1, 2):
+            to += [(0, 1)]
+        if rb == 1 and ra in (0, 3):
+            to += [(0, 3)]
+        for da, db in to:
+            piece_copy(p, *along(da, db)).start()
+        piece_copy(p, me, y * 2 + (1 - k)).start()
+
+    def wait_piece(p):
+        remote(
+            pieces.at[p], pieces.at[p], ss_piece, rs_piece.at[p], me, y * 2 + (1 - k)
+        ).wait_recv()
+
+    for j in range(4):
+
+        @pl.when(2 * j + k != z)
+        def _():
+            remote(
+                pieces.at[first, j],
+                pieces.at[first, j],
+                ss_z.at[2 * j + k],
+                rs_z.at[j],
+                x * Z + 2 * j + k,
+                feat,
+            ).wait_recv()
+
+    piece_sends(0, 0)
     pl.semaphore_wait(far, Z - 1)
 
-    def send_codes(dz, carry):
-        for dx in (1, 3, 2):
+    for dz in (0, 4, 3, 5, 2, 6, 1, 7):
+        for dx in (1, 3):
             codes_copy(dx, dz).start()
-        return carry
-
-    lax.fori_loop(0, Z, send_codes, 0)
 
     def sums_copy(j):
         to = lax.rem(me + j, CLIENTS)
@@ -261,11 +305,8 @@
             axis=1,
         )
 
-        def send_sums(j, carry):
+        for j in range(1, CLIENTS):
             sums_copy(j).start()
-            return carry
-
-        lax.fori_loop(1, CLIENTS, send_sums, 0)
 
     def meet_nodes():
         many(sums, CLIENTS - 1, ss_sums, rs_sums).wait_recv()
@@ -273,69 +314,8 @@
         for j in range(1, FEATS):
             node_copy(j).start()
 
-    def order(t):
-        code = 0
-        for i, (ra, rb) in enumerate(ORDER):
-            code = code + jnp.where(t == i, 4 * ra + rb, 0)
-        return lax.div(code, 4), lax.rem(code, 4)
-
-    def along(da, db):
-        ax = da * (1 - k) + db * k
-        ay = da * k + db * (1 - k)
-        return (lax.rem(x + ax, X)) * Z + z, (lax.rem(y + ay, Y)) * 2 + k
-
-    def piece_copy(p, client, to_feat):
-        return remote(pieces.at[p], pieces.at[p], ss_piece, rs_piece.at[p], client, to_feat)
-
-    def piece_sends(ra, rb):
-        p = piece_at(ra, rb, k)[2]
-        piece_copy(p, me, y * 2 + (1 - k)).start()
-
-        @pl.when((rb == 0) & (ra == 0))
-        def _():
-            for d in (1, 3):
-                piece_copy(p, *along(d, 0)).start()
-
-        @pl.when((rb == 0) & (ra == 1))
-        def _():
-            piece_copy(p, *along(3, 0)).start()
-
-        @pl.when(rb == 0)
-        def _():
-            for d in (1, 3):
-                piece_copy(p, *along(0, d)).start()
-
-        @pl.when((rb == 3) & ((ra == 1) | (ra == 2)))
-        def _():
-            piece_copy(p, *along(0, 1)).start()
-
-        @pl.when((rb == 1) & ((ra == 0) | (ra == 3)))
-        def _():
-            piece_copy(p, *along(0, 3)).start()
-
-    def wait_piece(p):
-        remote(
-            pieces.at[p], pieces.at[p], ss_piece, rs_piece.at[p], me, y * 2 + (1 - k)
-        ).wait_recv()
-
-    for j in range(4):
-
-        @pl.when(2 * j + k != z)
-        def _():
-            remote(
-                pieces.at[first, j],
-                pieces.at[first, j],
-                ss_z.at[2 * j + k],
-                rs_z.at[j],
-                x * Z + 2 * j + k,
-                feat,
-            ).wait_recv()
-
-    piece_sends(0, 0)
-
-    def event(t):
-        ra, rb = order(t)
-        wait_piece(piece_at(ra, rb, k)[2])
+    def event(ra, rb):
+        wait_piece(own_piece(ra, rb))
         piece_sends(ra, rb)
 
     acc[...] = jnp.zeros_like(acc)
@@ -349,15 +329,12 @@
         code_list = []
         node_list = []
         stat_list = []
-        for ra, rb in steps:
+        for dx, dy in steps:
             for which in range(2):
                 par = k * (1 - which) + (1 - k) * which
-                px, quarter, p = piece_at(ra, rb, par)
-
-                @pl.when(((1 - par) * rb + par * ra) == 0)
-                def _():
+                px, quarter, p = piece_at(dx, dy, par)
+                if dy == 0:
                     wait_codes(px, par)
-
                 if which == 1:
                     wait_piece(p)
                 half = lax.div(quarter, 2)
@@ -382,30 +359,27 @@
         )
         acc[...] += lax.dot_general(spread, onehot, CONTRACT_LAST, preferred_element_type=F32)
 
-    compute([(0, 0)])
-    client_sums()
-    event(1)
-    event(2)
-
-    def step(t, carry):
-        @pl.when(t < 7)
-        def _():
-            event(2 * t + 1)
-            event(2 * t + 2)
-
-        @pl.when(t == 7)
-        def _():
-            event(15)
-
-        @pl.when(t == 5)
-        def _():
+    for what, *at in PLAN:
+        if what == "sums":
+            client_sums()
+        elif what == "near":
+            dx, dy = at
+            wait_piece(piece_at(dx, dy, k)[2])
+            for core in range(2):
+
+                @pl.when(k == core)
+                def _():
+                    piece_sends(*((dx, dy) if core == 0 else (dy, dx)))
+
+        elif what == "codes":
+            for dz in (0, 4, 3, 5, 2, 6, 1, 7):
+                codes_copy(2, dz).start()
+        elif what == "meet":
             meet_nodes()
-
-        compute([order(2 * t - 1), order(2 * t)])
-        return carry
-
-    lax.fori_loop(1, 8, step, 0)
-    compute([order(15 + 0 * k)])
+        elif what == "take":
+            event(*at)
+        else:
+            compute(list(zip(at[::2], at[1::2])))
 
     many(node_sums, FEATS - 1, ss_node, rs_node).wait_recv()
     total = jnp.concatenate([node_sums[n] for n in range(NODES)], axis=0)

time: 45.5 us -> 42 us (0.923)
  Pallas kernels: 42.9 us -> 39.4 us
    pallas_call x1, Pallas kernels: 42.9 us -> 39.4 us  [local(): pl.pallas_call(kernel, out_shape=(jax.ShapeDtypeStruct((NODES, OWNED, BIN...]
where the time goes in v3:
time: 42 us; the launch traced here: 41.9 us
  Pallas kernels  39.4 us (94%)
  local copies, waits for them, and re-layouts  1.85 us (4%)
  between operations  0.64 us (2%)
    pallas_call x1, Pallas kernels, local(): pl.pallas_call(kernel, out_shape=(jax.ShapeDtypeStruct((NODES, OWNED, BIN...  39.4 us
    unnamed x3, local copies, waits for them, and re-layouts  1.85 us

profile of v3, /device:TPU:1, one launch (start us, length us, event | category | flops | bytes accessed | tf_op | source)
XLA Modules:
  0.0 41.9 jit_solution(17995888968037050199)
XLA Ops:
  0.6 39.4 %level.1 = (f32[8,2,256]{2,1,0:T(2,128)S(1)}, f32[16,16]{1,0:T(8,128)S(1)}, f32[16,1536]{1,0:T(8,128)S(1)}) custom-call(s32[8]{0:T(128)} %feature_in.1, s32[8]{0:T(128)} %bin_in.1, s32[64,1536]{1,0:T(8,128)} %codes_in.1, s32[12,128]{1,0:T(8,128)} %bitcast.1, f32[16,1536]{1,0:T(8,128)} %margins_in.1, f32[16,1536]{1,0:T(8,128)} %labels_in.1), custom_call_target="tpu_custom_call" | custom-call | tf_op jit(solution)/shard_map/level/pallas_call | solution.py:434
  40.0 0.6 %copy.12 = f32[8,2,256]{2,1,0:T(2,128)} copy(f32[8,2,256]{2,1,0:T(2,128)S(1)} %get-tuple-element.6) | data formatting | bytes 32768
  40.6 0.6 %copy.13 = f32[16,16]{1,0:T(8,128)} copy(f32[16,16]{1,0:T(8,128)S(1)} %get-tuple-element.7) | data formatting | bytes 2048
  41.2 0.6 %copy.14 = f32[16,1536]{1,0:T(8,128)} copy(f32[16,1536]{1,0:T(8,128)S(1)} %get-tuple-element.8) | data formatting | bytes 196608

commit v4 on v3

--- a/solution.py
+++ b/solution.py
@@ -23,12 +23,11 @@
 reg_lambda = 1.0
 step_eta = 0.5
 PLAN = (
-    ("add", 0, 0), ("sums",), ("near", 0, 1), ("near", 0, 3), ("near", 1, 0), ("near", 3, 0), ("codes",), ("add", 0, 1, 0, 3),
-    ("take", 2, 0), ("add", 1, 0, 3, 0), ("take", 1, 1),
-    ("take", 1, 3), ("take", 3, 1), ("take", 3, 3), ("take", 0, 2), ("add", 0, 2, 2, 0),
-    ("add", 1, 1, 1, 3), ("take", 2, 1), ("take", 2, 3), ("add", 3, 1, 3, 3), ("take", 1, 2),
-    ("take", 3, 2), ("meet",), ("add", 1, 2, 3, 2), ("take", 2, 2), ("add", 2, 1, 2, 3),
-    ("add", 2, 2),
+    ("add", 0, 0), ("sums",), ("near", 0, 1), ("near", 0, 3), ("near", 1, 0), ("near", 3, 0),
+    ("codes",), ("add", 0, 1, 0, 3), ("add", 1, 0, 3, 0), ("take", 2, 0), ("take", 1, 1), ("take", 1, 3),
+    ("take", 3, 1), ("take", 3, 3), ("add", 1, 1, 1, 3), ("take", 0, 2), ("add", 3, 1, 3, 3),
+    ("take", 2, 1), ("take", 2, 3), ("add", 0, 2, 2, 0), ("take", 1, 2), ("take", 3, 2),
+    ("meet",), ("add", 1, 2, 3, 2), ("take", 2, 2), ("add", 2, 1, 2, 3), ("add", 2, 2),
 )
 CONTRACT_LAST = (((1,), (1,)), ((), ()))
 
@@ -427,17 +426,29 @@
     many(pieces, 2 * X * Y - 1, ss_piece, rs_piece.at[0]).wait_send()
 
 
+def put_out(gains, leaf, new, gains_out, leaf_out, new_out, sems):
+    copies = [
+        pltpu.make_async_copy(src, dst, sems.at[i])
+        for i, (src, dst) in enumerate(((gains, gains_out), (leaf, leaf_out), (new, new_out)))
+    ]
+    for copy in copies:
+        copy.start()
+    for copy in copies:
+        copy.wait()
+
+
 def local(bin_codes, node_ids, margins, labels, split_feature, split_bin):
     vmem = pl.BlockSpec(memory_space=pltpu.VMEM)
     hbm = pl.BlockSpec(memory_space=pltpu.HBM)
     dma = pltpu.SemaphoreType.DMA
-    return pl.pallas_call(
+    shapes = (
+        jax.ShapeDtypeStruct((NODES, OWNED, BINS), F32),
+        jax.ShapeDtypeStruct((2 * NODES, TARGETS), F32),
+        jax.ShapeDtypeStruct((TARGETS, ROWS), F32),
+    )
+    outs = pl.pallas_call(
         kernel,
-        out_shape=(
-            jax.ShapeDtypeStruct((NODES, OWNED, BINS), F32),
-            jax.ShapeDtypeStruct((2 * NODES, TARGETS), F32),
-            jax.ShapeDtypeStruct((TARGETS, ROWS), F32),
-        ),
+        out_shape=shapes,
         in_specs=[hbm] * 6,
         out_specs=(vmem, vmem, vmem),
         scratch_shapes=[
@@ -477,6 +488,15 @@
         ),
         name="level",
     )(*[pltpu.with_memory_space_constraint(a, pltpu.HBM) for a in (split_feature, split_bin, bin_codes, node_ids.reshape(ROWS // 128, 128), margins, labels)])
+    return pl.pallas_call(
+        put_out,
+        out_shape=shapes,
+        in_specs=[vmem] * 3,
+        out_specs=(hbm,) * 3,
+        scratch_shapes=[dma((3,))],
+        compiler_params=pltpu.CompilerParams(vmem_limit_bytes=4 << 20),
+        name="put_out",
+    )(*outs)
 
 
 def solution(mesh):

time: 42 us -> 40.4 us (0.962)
  local copies, waits for them, and re-layouts: 1.85 us -> 0 us
    unnamed x3 -> x0, local copies, waits for them, and re-layouts: 1.85 us -> none
    pallas_call x1 -> x2, Pallas kernels: 39.4 us -> 39.5 us  [the longest x1 38.8 us: local(): pl.pallas_call(kernel, out_shape=shapes, in_specs=[hbm] * 6, out_specs=(v...]
where the time goes in v4:
time: 40.4 us; the launch traced here: 40.3 us
  Pallas kernels  39.5 us (98%)
  between operations  0.8 us (2%)
    pallas_call x1, Pallas kernels, local(): pl.pallas_call(kernel, out_shape=shapes, in_specs=[hbm] * 6, out_specs=(v...  38.8 us

profile of v4, /device:TPU:1, one launch (start us, length us, event | category | flops | bytes accessed | tf_op | source)
XLA Modules:
  0.0 40.3 jit_solution(11419190159197221002)
XLA Ops:
  0.6 38.8 %level.1 = (f32[8,2,256]{2,1,0:T(2,128)S(1)}, f32[16,16]{1,0:T(8,128)S(1)}, f32[16,1536]{1,0:T(8,128)S(1)}) custom-call(s32[8]{0:T(128)} %feature_in.1, s32[8]{0:T(128)} %bin_in.1, s32[64,1536]{1,0:T(8,128)} %codes_in.1, s32[12,128]{1,0:T(8,128)} %bitcast.1, f32[16,1536]{1,0:T(8,128)} %margins_in.1, f32[16,1536]{1,0:T(8,128)} %labels_in.1), custom_call_target="tpu_custom_call" | custom-call | tf_op jit(solution)/shard_map/level/pallas_call | solution.py:449
  39.4 0.7 %put_out.1 = (f32[8,2,256]{2,1,0:T(2,128)}, f32[16,16]{1,0:T(8,128)}, f32[16,1536]{1,0:T(8,128)}) custom-call(f32[8,2,256]{2,1,0:T(2,128)S(1)} %get-tuple-element.6.gains, f32[16,16]{1,0:T(8,128)S(1)} %get-tuple-element.7.leaf, f32[16,1536]{1,0:T(8,128)S(1)} %get-tuple-element.8.new), custom_call_target="tpu_custom_call" | custom-call | tf_op jit(solution)/shard_map/put_out/pallas_call | solution.py:491

commit v5 on v4

--- a/solution.py
+++ b/solution.py
@@ -24,10 +24,10 @@
 step_eta = 0.5
 PLAN = (
     ("add", 0, 0), ("sums",), ("near", 0, 1), ("near", 0, 3), ("near", 1, 0), ("near", 3, 0),
-    ("codes",), ("add", 0, 1, 0, 3), ("add", 1, 0, 3, 0), ("take", 2, 0), ("take", 1, 1), ("take", 1, 3),
+    ("add", 0, 1, 0, 3), ("codes",), ("add", 1, 0, 3, 0), ("take", 2, 0), ("take", 1, 1), ("take", 1, 3),
     ("take", 3, 1), ("take", 3, 3), ("add", 1, 1, 1, 3), ("take", 0, 2), ("add", 3, 1, 3, 3),
-    ("take", 2, 1), ("take", 2, 3), ("add", 0, 2, 2, 0), ("take", 1, 2), ("take", 3, 2),
-    ("meet",), ("add", 1, 2, 3, 2), ("take", 2, 2), ("add", 2, 1, 2, 3), ("add", 2, 2),
+    ("take", 2, 1), ("take", 2, 3), ("meet",), ("add", 0, 2, 2, 0), ("take", 1, 2), ("take", 3, 2),
+    ("add", 1, 2, 3, 2), ("leaf",), ("take", 2, 2), ("add", 2, 1, 2, 3), ("add", 2, 2),
 )
 CONTRACT_LAST = (((1,), (1,)), ((), ()))
 
@@ -358,6 +358,26 @@
         )
         acc[...] += lax.dot_general(spread, onehot, CONTRACT_LAST, preferred_element_type=F32)
 
+    def finish_leaves():
+        many(node_sums, FEATS - 1, ss_node, rs_node).wait_recv()
+        total = jnp.concatenate([node_sums[n] for n in range(NODES)], axis=0)
+        left = total[:, :CH]
+        whole = total[:, CH : 2 * CH]
+        right = whole - left
+        left_weight = -left[:, :TARGETS] / (left[:, TARGETS:] + reg_lambda)
+        right_weight = -right[:, :TARGETS] / (right[:, TARGETS:] + reg_lambda)
+        rows = []
+        for n in range(NODES):
+            rows.append(left_weight[n : n + 1])
+            rows.append(right_weight[n : n + 1])
+        weights = jnp.concatenate(rows, axis=0)
+        leaf_out[...] = weights
+        columns = jnp.concatenate([weights, jnp.zeros((2 * NODES, 128 - TARGETS), F32)], axis=1).T
+        child_iota = lax.broadcasted_iota(jnp.int32, (2 * NODES, ROWS), 0)
+        child_mask = jnp.where(child_iota == child_ref[...], 1.0, 0.0).astype(BF16)
+        lookup = dot3(columns[:TARGETS, :], child_mask)
+        margins_out[...] = margins[...] + step_eta * lookup
+
     for what, *at in PLAN:
         if what == "sums":
             client_sums()
@@ -375,29 +395,12 @@
                 codes_copy(2, dz).start()
         elif what == "meet":
             meet_nodes()
+        elif what == "leaf":
+            finish_leaves()
         elif what == "take":
             event(*at)
         else:
             compute(list(zip(at[::2], at[1::2])))
-
-    many(node_sums, FEATS - 1, ss_node, rs_node).wait_recv()
-    total = jnp.concatenate([node_sums[n] for n in range(NODES)], axis=0)
-    left = total[:, :CH]
-    whole = total[:, CH : 2 * CH]
-    right = whole - left
-    left_weight = -left[:, :TARGETS] / (left[:, TARGETS:] + reg_lambda)
-    right_weight = -right[:, :TARGETS] / (right[:, TARGETS:] + reg_lambda)
-    rows = []
-    for n in range(NODES):
-        rows.append(left_weight[n : n + 1])
-        rows.append(right_weight[n : n + 1])
-    weights = jnp.concatenate(rows, axis=0)
-    leaf_out[...] = weights
-    columns = jnp.concatenate([weights, jnp.zeros((2 * NODES, 128 - TARGETS), F32)], axis=1).T
-    child_iota = lax.broadcasted_iota(jnp.int32, (2 * NODES, ROWS), 0)
-    child_mask = jnp.where(child_iota == child_ref[...], 1.0, 0.0).astype(BF16)
-    lookup = dot3(columns[:TARGETS, :], child_mask)
-    margins_out[...] = margins[...] + step_eta * lookup
 
     row_bin = lax.broadcasted_iota(jnp.int32, (BINS, BINS), 0)
     col_bin = lax.broadcasted_iota(jnp.int32, (BINS, BINS), 1)

time: 40.4 us -> 40.4 us (level)
  no operation moved by 1% of the time
where the time goes in v5:
time: 40.4 us; the launch traced here: 40.3 us
  Pallas kernels  39.5 us (98%)
  between operations  0.8 us (2%)
    pallas_call x1, Pallas kernels, local(): pl.pallas_call(kernel, out_shape=shapes, in_specs=[hbm] * 6, out_specs=(v...  38.8 us

profile of v5, /device:TPU:1, one launch (start us, length us, event | category | flops | bytes accessed | tf_op | source)
XLA Modules:
  0.0 40.3 jit_solution(5610006977932339953)
XLA Ops:
  0.6 38.8 %level.1 = (f32[8,2,256]{2,1,0:T(2,128)S(1)}, f32[16,16]{1,0:T(8,128)S(1)}, f32[16,1536]{1,0:T(8,128)S(1)}) custom-call(s32[8]{0:T(128)} %feature_in.1, s32[8]{0:T(128)} %bin_in.1, s32[64,1536]{1,0:T(8,128)} %codes_in.1, s32[12,128]{1,0:T(8,128)} %bitcast.1, f32[16,1536]{1,0:T(8,128)} %margins_in.1, f32[16,1536]{1,0:T(8,128)} %labels_in.1), custom_call_target="tpu_custom_call" | custom-call | tf_op jit(solution)/shard_map/level/pallas_call | solution.py:452
  39.5 0.7 %put_out.1 = (f32[8,2,256]{2,1,0:T(2,128)}, f32[16,16]{1,0:T(8,128)}, f32[16,1536]{1,0:T(8,128)}) custom-call(f32[8,2,256]{2,1,0:T(2,128)S(1)} %get-tuple-element.6.gains, f32[16,16]{1,0:T(8,128)S(1)} %get-tuple-element.7.leaf, f32[16,1536]{1,0:T(8,128)S(1)} %get-tuple-element.8.new), custom_call_target="tpu_custom_call" | custom-call | tf_op jit(solution)/shard_map/put_out/pallas_call | solution.py:494
